TPU v7x, 32 devices: a whole 2x2x4 slice. The times are simulated.
32 devices in a mesh: sector: 4 (over y, x), term: 8 (over z, core).
Axes of the slice: x: 2, y: 2, z: 4, core: 2. Of those that a mesh axis runs over, the one named last changes fastest.
Arguments:
- wavefunction: float32 [4, 256, 256], P('sector'), may hold values from -6 to 6
- left_env: float32 [384, 256, 256], P(('sector', 'term')), may hold values from -0.0390625 to 0.0390625
- right_env: float32 [384, 256, 256], P(('sector', 'term')), may hold values from -0.375 to 0.375
- in_sector: int32 [384], P(('sector', 'term')), may hold values from 0 to 3
- out_sector: int32 [384], P(('sector', 'term')), may hold values from 0 to 3
- precond: float32 [4, 256, 256], P('sector'), may hold values from 2 to 4
- shifts: float32 [2], replicated, may hold values from 0.2 to 1
Outputs:
- corrected: float32 [4, 256, 256], P('sector')
- residual_norms: float32 [2], replicated
All inputs are finite; a program needn't handle non-finite values.
Results may differ from a plain program's by a relative error of at most 0.0001.
Values sent between devices are 32-bit elements; how exact they have to be, the bound alone decides.
A program may use at most 64 MiB of HBM per device.

v0:
```python
import jax
import jax.numpy as jnp
from jax import lax
from jax.sharding import PartitionSpec as P

ITERS = 2


def apply_tasks(full, left_env, right_env, in_sector, out_sector):

    def one_task(total, item):
        left, right, source, target = item
        block = lax.dynamic_index_in_dim(full, source, 0, keepdims=False)
        middle = jnp.dot(
            left, block, precision=lax.Precision.HIGHEST, preferred_element_type=jnp.float32
        )
        result = jnp.dot(
            middle, right, precision=lax.Precision.HIGHEST, preferred_element_type=jnp.float32
        )
        current = lax.dynamic_index_in_dim(total, target, 0, keepdims=False)
        total = lax.dynamic_update_index_in_dim(total, current + result, target, 0)
        return (total, None)

    start = jnp.zeros(full.shape, jnp.float32)
    total, _ = lax.scan(one_task, start, (left_env, right_env, in_sector, out_sector))
    return total


def correction(sigma, psi, precond, shift):
    residual = sigma - shift * psi
    updated = psi - residual / (precond - shift)
    return (updated, jnp.sum(residual * residual), jnp.sum(updated * updated))


def per_device(wavefunction, left_env, right_env, in_sector, out_sector, precond, shifts):
    full = lax.all_gather(wavefunction, "sector", axis=0, tiled=True)
    norms = []
    psi = wavefunction
    count = lax.axis_size("sector") * psi.size
    for step in range(ITERS):
        partial_value = apply_tasks(full, left_env, right_env, in_sector, out_sector)
        owned = lax.psum_scatter(partial_value, "sector", scatter_dimension=0, tiled=True)
        sigma = lax.psum(owned, "term")
        updated, res_sq, upd_sq = correction(sigma, psi, precond, shifts[step])
        res_total, upd_total = lax.psum((res_sq, upd_sq), "sector")
        norms.append(jnp.sqrt(res_total))
        psi = updated / jnp.sqrt(upd_total / count + 1e-06)
        if step + 1 < ITERS:
            full = lax.all_gather(psi, "sector", axis=0, tiled=True)
    return (psi, jnp.stack(norms))


def solution(mesh):
    placed = (
        P("sector", None, None),
        P(("sector", "term"), None, None),
        P(("sector", "term"), None, None),
        P(("sector", "term")),
        P(("sector", "term")),
        P("sector", None, None),
        P(),
    )
    return jax.shard_map(
        per_device,
        mesh=mesh,
        in_specs=placed,
        out_specs=(P("sector", None, None), P()),
        check_vma=False,
    )
```

profile of v0, /device:TPU:0, one launch (start us, length us, event | category | flops | bytes accessed | tf_op | source)
XLA Modules:
  0.0 478.9 jit_solution(9953802204697645868)
XLA Ops:
  7.9 31.1 %all-gather.3.cloned.1.call-done = f32[4,256,256]{2,1,0:T(8,128)} async-done(((f32[1,256,256]{2,1,0:T(8,128)}), f32[4,256,256]{2,1,0:T(8,128)}) %all-gather.3.cloned.1.call-update) | async-done | bytes 1048592 | tf_op jit(solution)/shard_map/all_gather | solution.py:36
  39.2 110.3 %while.20 = (s32[]{:T(128)}, f32[4,256,256]{2,1,0:T(8,128)S(1)}, s32[12]{0:T(128)}, f32[12,256,256]{2,1,0:T(8,128)}, s32[12]{0:T(128)}, /*index=5*/f32[4,256,256...) while((s32[]{:T(128)}, f32[4,256,256]{2,1,0:T(8,128)S(1)}, s32[12]{0:T(128)}, ...), condition=%wide.region_1.2_spmd, body=%wide.region_0.1_spmd.sunk | while | flops 402718720 | bytes 2360525 | solution.py:25
  39.2 1.3 dynamic_slice.82
  42.4 1.4 fusion.41
  43.9 1.2 dynamic_slice.81
  47.1 1.3 fusion.42
  51.6 1.4 fusion.41
  53.1 1.2 dynamic_slice.81
  56.3 1.3 fusion.42
  60.8 1.4 fusion.41
  65.5 1.3 fusion.42
  70.0 1.4 fusion.41
  71.4 1.2 dynamic_slice.81
  74.7 1.3 fusion.42
  79.2 1.4 fusion.41
  83.8 1.3 fusion.42
  88.4 1.4 fusion.41
  93.0 1.3 fusion.42
  97.6 1.4 fusion.41
  102.2 1.3 fusion.42
  106.8 1.4 fusion.41
  111.4 1.3 fusion.42
  116.0 1.4 fusion.41
  120.6 1.3 fusion.42
  125.2 1.4 fusion.41
  129.8 1.3 fusion.42
  134.4 1.4 fusion.41
  139.0 1.3 fusion.42
  143.5 1.4 fusion.41
  148.2 1.3 fusion.42
  150.6 28.0 %reduce-scatter.7.cloned.1.call-done = f32[1,256,256]{2,1,0:T(8,128)} async-done(((f32[4,256,256]{2,1,0:T(8,128)}), f32[1,256,256]{2,1,0:T(8,128)}) %reduce-scatter.7.cloned.1.call-update) | async-done | bytes 262160
  179.3 57.1 %all-reduce.6.cloned.1.call-done = f32[1,256,256]{2,1,0:T(8,128)} async-done(((f32[1,256,256]{2,1,0:T(8,128)}), f32[1,256,256]{2,1,0:T(8,128)}) %all-reduce.6.cloned.1.call-update) | async-done | bytes 262160 | tf_op jit(solution)/shard_map/psum | solution.py:43
  236.4 2.4 multiply_reduce_fusion.3
  238.8 10.4 %psum.43 = f32[]{:T(128)} all-reduce(f32[]{:T(128)} %get-tuple-element.111), channel_id=1, replica_groups=mesh['sector'=4,'term'=8] {'sector'}, use_global_device_ids=true, to_apply=%region_5.6 | all-reduce | flops 1 | bytes 8 | tf_op jit(solution)/shard_map/psum | solution.py:45
  250.7 23.8 %all-gather.5.cloned.1.call-done = f32[4,256,256]{2,1,0:T(8,128)} async-done(((f32[1,256,256]{2,1,0:T(8,128)}), f32[4,256,256]{2,1,0:T(8,128)}) %all-gather.5.cloned.1.call-update) | async-done | bytes 1048592 | tf_op jit(solution)/shard_map/all_gather | solution.py:49
  274.7 94.6 %while.21 = (s32[]{:T(128)}, f32[4,256,256]{2,1,0:T(8,128)S(1)}, s32[12]{0:T(128)S(1)}, f32[12,256,256]{2,1,0:T(8,128)}, s32[12]{0:T(128)S(1)}, /*index=5*/f32[4...) while((s32[]{:T(128)}, f32[4,256,256]{2,1,0:T(8,128)S(1)}, ...), condition=%wide.region_7.8_spmd, body=%wide.region_6.7_spmd.sunk | while | flops 402718720 | bytes 2360525 | solution.py:25
  277.2 1.4 fusion.47
  281.2 1.3 fusion.48
  285.1 1.4 fusion.47
  289.1 1.3 fusion.48
  293.0 1.4 fusion.47
  296.9 1.3 fusion.48
  300.8 1.4 fusion.47
  304.8 1.3 fusion.48
  308.7 1.4 fusion.47
  312.7 1.3 fusion.48
  316.6 1.4 fusion.47
  320.6 1.3 fusion.48
  324.5 1.4 fusion.47
  328.5 1.3 fusion.48
  332.4 1.4 fusion.47
  336.4 1.3 fusion.48
  340.2 1.4 fusion.47
  344.2 1.3 fusion.48
  348.1 1.4 fusion.47
  352.1 1.3 fusion.48
  356.0 1.4 fusion.47
  360.0 1.3 fusion.48
  363.9 1.4 fusion.47
  367.9 1.3 fusion.48
  370.3 28.0 %reduce-scatter.9.cloned.1.call-done = f32[1,256,256]{2,1,0:T(8,128)} async-done(((f32[4,256,256]{2,1,0:T(8,128)}), f32[1,256,256]{2,1,0:T(8,128)}) %reduce-scatter.9.cloned.1.call-update) | async-done | bytes 262160
  398.4 57.6 %all-reduce.8.cloned.1.call-done = f32[1,256,256]{2,1,0:T(8,128)} async-done(((f32[1,256,256]{2,1,0:T(8,128)}), f32[1,256,256]{2,1,0:T(8,128)}) %all-reduce.8.cloned.1.call-update) | async-done | bytes 262160 | tf_op jit(solution)/shard_map/psum | solution.py:43
  455.9 2.2 multiply_reduce_fusion.2
  458.2 10.5 %all-reduce.2 = (f32[]{:T(128)}, f32[]{:T(128)}, f32[]{:T(128)}) all-reduce(f32[]{:T(128)} %get-tuple-element.109, f32[]{:T(128)} %get-tuple-element.114, f32[]{:T(128)} %get-tuple-element.113), channel_id=1, replica_groups=mesh['sector'=4,'term'=8] {'sector'}, use_global_device_ids=true, to_apply=%region_11.12 | all-reduce | flops 3 | bytes 24 | tf_op jit(solution)/shard_map/psum | solution.py:45
  (100 shorter events, 45.3 us)
Async XLA Ops:
  7.2 31.9 %all-gather.3.cloned.1.call-start = ((), (), s32[]{:S(2)}) async-start(), calls=%async_computation.2 | async-start | bytes 1310720 | tf_op jit(solution)/shard_map/all_gather | solution.py:36
  7.9 170.7 %reduce-scatter.7.cloned.1.call-start = ((), (), s32[]{:S(2)}) async-start(), calls=%async_computation.6 | async-start | bytes 1310720
  39.2 139.6 %copy-start.4 = (f32[2]{0:T(128)S(1)}, f32[2]{0:T(128)}, u32[]{:S(2)}) copy-start(f32[2]{0:T(128)} %param.17) | copy-start | bytes 28
  39.2 197.2 %copy-start.2 = (f32[1,256,256]{2,1,0:T(8,128)S(1)}, f32[1,256,256]{2,1,0:T(8,128)}, u32[]{:S(2)}) copy-start(f32[1,256,256]{2,1,0:T(8,128)} %param.11) | copy-start | bytes 786436
  39.2 197.2 %copy-start.3 = (f32[1,256,256]{2,1,0:T(8,128)S(1)}, f32[1,256,256]{2,1,0:T(8,128)}, u32[]{:S(2)}) copy-start(f32[1,256,256]{2,1,0:T(8,128)} %param.16) | copy-start | bytes 786436
  149.5 1.0 copy-start.1
  149.6 125.1 %copy-start.5 = (s32[12]{0:T(128)S(1)}, s32[12]{0:T(128)}, u32[]{:S(2)}) copy-start(s32[12]{0:T(128)} %get-tuple-element.289) | copy-start | bytes 148
  149.6 125.1 %copy-start.6 = (s32[12]{0:T(128)S(1)}, s32[12]{0:T(128)}, u32[]{:S(2)}) copy-start(s32[12]{0:T(128)} %get-tuple-element.290) | copy-start | bytes 148
  150.5 85.9 %all-reduce.6.cloned.1.call-start = ((), (), s32[]{:S(2)}) async-start(), calls=%async_computation.3 | async-start | bytes 524288 | tf_op jit(solution)/shard_map/psum | solution.py:43
  178.7 95.9 %all-gather.5.cloned.1.call-start = ((), (), s32[]{:S(2)}) async-start(), calls=%async_computation.4 | async-start | bytes 1310720 | tf_op jit(solution)/shard_map/all_gather | solution.py:49
  250.7 147.7 %reduce-scatter.9.cloned.1.call-start = ((), (), s32[]{:S(2)}) async-start(), calls=%async_computation.7 | async-start | bytes 1310720
  369.2 1.0 copy-start
  370.2 85.7 %all-reduce.8.cloned.1.call-start = ((), (), s32[]{:S(2)}) async-start(), calls=%async_computation.5 | async-start | bytes 524288 | tf_op jit(solution)/shard_map/psum | solution.py:43
Sparse Core Ops, SparseCore 0:
  9.8 29.2 all-gather.2
  150.7 27.9 reduce-scatter.6
  181.0 55.4 all-reduce.5
  250.8 23.7 all-gather.4
  370.4 27.9 reduce-scatter.8
  400.5 55.4 all-reduce.7
where the time goes:
time: 482 us; the launch traced here: 479 us
  waiting for transfers between devices  226 us (47%)
  loops' own time  94.2 us (20%)
  matrix products  66.1 us (14%)
  local copies, waits for them, and re-layouts  47.3 us (10%)
  blocking collectives  20.9 us (4%)
  between operations  17 us (4%)
  other arithmetic  6.63 us (1%)
    psum x2, waiting for transfers between devices, per_device(): sigma = lax.psum(owned, 'term')  115 us
    another operation x2, loops' own time, apply_tasks(): lax.scan(one_task, start, (left_env, right_env, in_sector, out_sector))  94.2 us
    unnamed x8, waiting for transfers between devices  56.8 us
    dynamic_slice x48, local copies, waits for them, and re-layouts, apply_tasks(): lax.scan(one_task, start, (left_env, right_env, in_sector, out_sector))  44 us
    dot_general x24, matrix products, one_task(): jnp.dot(left, block, precision=lax.Precision.HIGHEST, preferred_element_t...  33.9 us
    dot_general x24, matrix products, one_task(): jnp.dot(middle, right, precision=lax.Precision.HIGHEST, preferred_element...  32.1 us
    all_gather x1, waiting for transfers between devices, per_device(): full = lax.all_gather(wavefunction, 'sector', axis=0, tiled=True)  31.1 us
    all_gather x1, waiting for transfers between devices, per_device(): full = lax.all_gather(psi, 'sector', axis=0, tiled=True)  23.8 us
  transfers between devices with their start and end apart: 6, of which 6 were waited for; matrix products, arithmetic and copies ran while one was open for 0% of the time, Pallas kernels for 0%

commit v1 on v0

v1 whole, which is shorter than its diff:
```python
import functools

import jax
import jax.numpy as jnp
from jax import lax
from jax.experimental import pallas as pl
from jax.experimental.pallas import tpu as pltpu
from jax.sharding import PartitionSpec as P

F32 = jnp.float32
BF16 = jnp.bfloat16


def split(x):
    hi = x.astype(BF16)
    return hi, (x - hi.astype(F32)).astype(BF16)


def rcopy(src, dst, sems, at, dev):
    return pltpu.make_async_remote_copy(
        src_ref=src,
        dst_ref=dst,
        send_sem=sems[0].at[at],
        recv_sem=sems[1].at[at],
        device_id=dev,
        device_id_type=pl.DeviceIdType.MESH,
    )


def each(start, stop, body):
    lax.fori_loop(start, stop, lambda i, _: (body(i), 0)[1], 0)


def kernel(
    S, T,
    in_s, out_s, shifts, wf, pre, left, right,
    out, norms,
    stage, env, full, fin, psi, mid, res, part, p1r, p2r, zsum, p3r, stat, zsr, xsr, csr,
    esem, *sems,
):
    g0, f0, p1, p2, p3, zg, xg, cg, zst, xst, cst = [
        (sems[2 * i], sems[2 * i + 1]) for i in range(len(sems) // 2)
    ]
    n_task, B = left.shape[0], wf.shape[-1]
    iters = norms.shape[0]
    Z, H = T // 2, B // 2
    R = H // Z
    count = S * B * B
    ms, mt = lax.axis_index("sector"), lax.axis_index("term")
    mz, mc = mt // 2, lax.rem(mt, 2)

    def sec_to(k):
        return lax.rem(ms + k, S)

    def sec_from(k):
        return lax.rem(ms + S - k, S)

    def z_to(k):
        return lax.rem(mz + k, Z)

    def z_from(k):
        return lax.rem(mz + Z - k, Z)

    def xy_dev(k):
        return (sec_to(k), mt)

    def z_dev(k):
        return (ms, z_to(k) * 2 + mc)

    core_dev = (ms, mz * 2 + 1 - mc)

    def half(c):
        return pl.ds(pl.multiple_of(c * H, H), H)

    def piece(c, z):
        return pl.ds(pl.multiple_of(c * H + z * R, R), R)

    def zrows(z):
        return pl.ds(pl.multiple_of(z * R, R), R)

    def env_copy(which, t):
        src = left if which == 0 else right
        return pltpu.make_async_copy(src.at[t], stage.at[which, t], esem.at[which, t])

    for which in range(2):
        each(0, n_task, lambda t: env_copy(which, t).start())

    barrier = pltpu.get_barrier_semaphore()

    def greet(dev):
        pl.semaphore_signal(barrier, inc=1, device_id=dev, device_id_type=pl.DeviceIdType.MESH)

    each(1, S, lambda k: greet(xy_dev(k)))
    each(1, Z, lambda k: greet(z_dev(k)))
    greet(core_dev)
    pl.semaphore_wait(barrier, S + Z - 1)

    def g0_copy(k):
        return rcopy(wf.at[0, half(mc)], full.at[0, ms, half(mc)], g0, k, xy_dev(k))

    def g0_in(k):
        here = full.at[0, sec_from(k), half(mc)]
        return rcopy(here, here, g0, k, xy_dev(k))

    def f0_copy(k):
        here = full.at[0, sec_from(k), half(mc)]
        return rcopy(here, here, f0, k, core_dev)

    def f0_in(k):
        here = full.at[0, sec_from(k), half(1 - mc)]
        return rcopy(here, here, f0, k, core_dev)

    each(1, S, lambda k: g0_copy(k).start())

    CH = 32

    def split_rows(load, dst, s):
        def rows(i):
            at = pl.ds(pl.multiple_of(i * CH, CH), CH)
            hi, lo = split(load(at))
            dst[0, s, at, :] = hi
            dst[1, s, at, :] = lo

        each(0, B // CH, rows)

    split_rows(lambda at: wf[0, at, :], psi, ms)

    for which in range(2):
        def convert(t):
            env_copy(which, t).wait()
            split_rows(lambda at: stage[which, t, at, :], env.at[which], t)

        each(0, n_task, convert)

    def forward0(k):
        g0_in(k).wait_recv()
        f0_copy(k).start()

    each(1, S, forward0)

    def arrive0(k):
        f0_in(k).wait_recv()
        s = sec_from(k)
        split_rows(lambda at: full[0, s, at, :], psi, s)

    each(1, S, arrive0)

    scale = None
    for it in range(iters):
        last = it == iters - 1

        def first(t):
            s = in_s[t]
            lh, ll = env[0, 0, t], env[0, 1, t]
            ph, plo = psi[0, s], psi[1, s]
            m = jnp.dot(
                jnp.concatenate([lh, ll, lh], axis=1),
                jnp.concatenate([ph, ph, plo], axis=0),
                preferred_element_type=F32,
            )
            mid[0, t], mid[1, t] = split(m)

        def second(t):
            mh, ml = mid[0, t], mid[1, t]
            rh, rl = env[1, 0, t], env[1, 1, t]
            res[t] = jnp.dot(
                jnp.concatenate([mh, ml, mh], axis=1),
                jnp.concatenate([rh, rh, rl], axis=0),
                preferred_element_type=F32,
            )

        each(0, n_task, first)
        each(0, n_task, second)

        def sums(s, c, dst, extra):
            coef = [jnp.where(out_s[t] == s, 1.0, 0.0).astype(F32) for t in range(n_task)]

            def rows(i):
                at = pl.ds(pl.multiple_of(i * CH, CH), CH)
                src = pl.ds(pl.multiple_of(c * H + i * CH, CH), CH)
                total = coef[0] * res[0, src, :]
                for t in range(1, n_task):
                    total = total + coef[t] * res[t, src, :]
                if extra:
                    total = total + p1r[it, s, at, :]
                part[dst, s, at, :] = total

            each(0, H // CH, rows)

        def p1_copy(s):
            return rcopy(part.at[1, s], p1r.at[it, s], p1, (it, s), core_dev)

        def to_partner(k):
            s = sec_to(k)
            sums(s, 1 - mc, 1, False)
            p1_copy(s).start()

        each(1, S + 1, to_partner)

        def p2_copy(j, k):
            return rcopy(
                part.at[0, sec_to(j), zrows(z_to(k))], p2r.at[it, j, k], p2, (it, j, k), xy_dev(j)
            )

        def to_owner(j):
            s = sec_to(j)
            p1_copy(s).wait_recv()
            sums(s, mc, 0, True)
            each(1, Z + 1, lambda k: p2_copy(j, lax.rem(k, Z)).start())

        each(1, S, to_owner)
        p1_copy(ms).wait_recv()
        sums(ms, mc, 0, True)

        def piece_sum(k):
            total = part[0, ms, zrows(z_to(k)), :]
            for j in range(1, S):
                p2_copy(j, k).wait_recv()
                total = total + p2r[it, j, k]
            return total

        def p3_copy(k):
            return rcopy(zsum.at[k], p3r.at[it, k], p3, (it, k), z_dev(k))

        def to_z(k):
            zsum[k] = piece_sum(k)
            p3_copy(k).start()

        each(1, Z, to_z)
        sigma = piece_sum(0)
        for k in range(1, Z):
            p3_copy(k).wait_recv()
            sigma = sigma + p3r[it, k]

        mine = piece(mc, mz)
        shift = shifts[it]
        prev = wf[0, mine, :] if it == 0 else full[it, ms, mine, :]
        residual = sigma - shift * prev
        updated = prev - residual / (pre[0, mine, :] - shift)
        res_sq = jnp.sum(residual * residual, axis=(0, 1), keepdims=True)
        upd_sq = jnp.sum(updated * updated, axis=(0, 1), keepdims=True)
        row = lax.broadcasted_iota(jnp.int32, (8, 128), 0)
        tile = jnp.where(row < 4, res_sq, upd_sq)

        def spot(s, at):
            return fin.at[at] if last else full.at[it + 1, s, at]

        if last:
            fin[mine, :] = updated
        else:
            full[it + 1, ms, mine, :] = updated
        stat[it, 0] = tile

        def zst_copy(k):
            return rcopy(stat.at[it, 0], zsr.at[it, k], zst, (it, k), z_dev(k))

        def xst_copy(j):
            return rcopy(stat.at[it, 1], xsr.at[it, j], xst, (it, j), xy_dev(j))

        cst_copy = rcopy(stat.at[it, 2], csr.at[it], cst, it, core_dev)

        def zg_copy(k):
            return rcopy(spot(ms, mine), spot(ms, mine), zg, (it, k), z_dev(k))

        def zg_in(k):
            here = spot(ms, piece(mc, z_from(k)))
            return rcopy(here, here, zg, (it, k), z_dev(k))

        def xg_copy(j, k):
            here = spot(ms, piece(mc, z_from(k)))
            return rcopy(here, here, xg, (it, j, k), xy_dev(j))

        def xg_in(j, k):
            here = spot(sec_from(j), piece(mc, z_from(k)))
            return rcopy(here, here, xg, (it, j, k), xy_dev(j))

        def cg_copy(j, k):
            here = spot(sec_from(j), piece(mc, z_from(k)))
            return rcopy(here, here, cg, (it, j, k), core_dev)

        def cg_in(j, k):
            here = spot(sec_from(j), piece(1 - mc, z_from(k)))
            return rcopy(here, here, cg, (it, j, k), core_dev)

        def spread(k):
            if not last:
                each(1, S, lambda j: xg_copy(j, k).start())
            cg_copy(0, k).start()

        each(1, Z, lambda k: zst_copy(k).start())
        each(1, Z, lambda k: zg_copy(k).start())
        spread(0)
        for k in range(1, Z):
            zst_copy(k).wait_recv()
            tile = tile + zsr[it, k]
        stat[it, 1] = tile
        each(1, S, lambda j: xst_copy(j).start())

        def relay_z(k):
            zg_in(k).wait_recv()
            spread(k)

        each(1, Z, relay_z)

        for j in range(1, S):
            xst_copy(j).wait_recv()
            tile = tile + xsr[it, j]
        stat[it, 2] = tile
        cst_copy.start()

        if not last:
            def relay_xy(k):
                def one(j):
                    xg_in(j, k).wait_recv()
                    cg_copy(j, k).start()

                each(1, S, one)

            each(0, Z, relay_xy)

        cst_copy.wait_recv()
        tile = tile + csr[it]
        res_all, upd_all = tile[0:1, 0:1], tile[4:5, 0:1]
        norm = jnp.sqrt(res_all)
        mean = upd_all / count
        if scale is None:
            scale = 1.0 / jnp.sqrt(mean + 1e-06)
        else:
            norm = norm * scale
            scale = scale / jnp.sqrt(scale * scale * mean + 1e-06)
        norms[it] = norm[0, 0]

        if last:
            each(0, Z, lambda k: cg_in(0, k).wait_recv())
            out[0] = fin[...] * scale
        else:
            def arrive(j):
                each(0, Z, lambda k: cg_in(j, k).wait_recv())
                s = sec_from(j)
                split_rows(lambda at: full[it + 1, s, at, :], psi, s)

            each(0, S, arrive)

        if it == 0:
            each(1, S, lambda k: g0_copy(k).wait_send())
            each(1, S, lambda k: f0_copy(k).wait_send())
        each(0, S, lambda s: p1_copy(s).wait_send())
        each(1, S, lambda j: each(0, Z, lambda k: p2_copy(j, k).wait_send()))
        each(1, Z, lambda k: p3_copy(k).wait_send())
        each(1, Z, lambda k: zst_copy(k).wait_send())
        each(1, S, lambda j: xst_copy(j).wait_send())
        cst_copy.wait_send()
        each(1, Z, lambda k: zg_copy(k).wait_send())
        each(0, Z, lambda k: cg_copy(0, k).wait_send())
        if not last:
            each(1, S, lambda j: each(0, Z, lambda k: xg_copy(j, k).wait_send()))
            each(1, S, lambda j: each(0, Z, lambda k: cg_copy(j, k).wait_send()))


def per_device(S, T, wavefunction, left_env, right_env, in_sector, out_sector, precond, shifts):
    n_task, B = left_env.shape[0], left_env.shape[-1]
    iters = shifts.shape[0]
    Z, H = T // 2, B // 2
    R = H // Z
    dma = pltpu.SemaphoreType.DMA
    vmem = pl.BlockSpec(memory_space=pltpu.VMEM)
    smem = pl.BlockSpec(memory_space=pltpu.SMEM)
    hbm = pl.BlockSpec(memory_space=pl.ANY)
    sem_shapes = [
        (S,), (S,), (iters, S), (iters, S, Z), (iters, Z), (iters, Z),
        (iters, S, Z), (iters, S, Z), (iters, Z), (iters, S), (iters,),
    ]
    return pl.pallas_call(
        functools.partial(kernel, S, T),
        out_shape=(
            jax.ShapeDtypeStruct((1, B, B), F32),
            jax.ShapeDtypeStruct((iters,), F32),
        ),
        in_specs=[smem, smem, smem, vmem, vmem, hbm, hbm],
        out_specs=(vmem, smem),
        scratch_shapes=[
            pltpu.VMEM((2, n_task, B, B), F32),
            pltpu.VMEM((2, 2, n_task, B, B), BF16),
            pltpu.VMEM((iters, S, B, B), F32),
            pltpu.VMEM((B, B), F32),
            pltpu.VMEM((2, S, B, B), BF16),
            pltpu.VMEM((2, n_task, B, B), BF16),
            pltpu.VMEM((n_task, B, B), F32),
            pltpu.VMEM((2, S, H, B), F32),
            pltpu.VMEM((iters, S, H, B), F32),
            pltpu.VMEM((iters, S, Z, R, B), F32),
            pltpu.VMEM((Z, R, B), F32),
            pltpu.VMEM((iters, Z, R, B), F32),
            pltpu.VMEM((iters, 3, 8, 128), F32),
            pltpu.VMEM((iters, Z, 8, 128), F32),
            pltpu.VMEM((iters, S, 8, 128), F32),
            pltpu.VMEM((iters, 8, 128), F32),
            dma((2, n_task)),
        ]
        + [dma(shape) for shape in sem_shapes for _ in range(2)],
        compiler_params=pltpu.CompilerParams(
            collective_id=0, has_side_effects=True, vmem_limit_bytes=62 * 1024 * 1024
        ),
    )(in_sector, out_sector, shifts, wavefunction, precond, left_env, right_env)


def solution(mesh):
    placed = (
        P("sector", None, None),
        P(("sector", "term"), None, None),
        P(("sector", "term"), None, None),
        P(("sector", "term")),
        P(("sector", "term")),
        P("sector", None, None),
        P(),
    )
    return jax.shard_map(
        functools.partial(per_device, mesh.shape["sector"], mesh.shape["term"]),
        mesh=mesh,
        in_specs=placed,
        out_specs=(P("sector", None, None), P()),
        check_vma=False,
    )
```

time: 482 us -> 79.8 us (0.17)
  waiting for transfers between devices: 226 us -> 0 us
  loops' own time: 94.2 us -> 0 us
  Pallas kernels: 0 us -> 76 us
  matrix products: 66.1 us -> 0 us
  local copies, waits for them, and re-layouts: 47.3 us -> 2.8 us
  blocking collectives: 20.9 us -> 0 us
  between operations: 17 us -> 0.64 us
  other arithmetic: 6.63 us -> 0 us
    psum x2 -> x0, waiting for transfers between devices: 115 us -> none  [per_device(): sigma = lax.psum(owned, 'term')]
    another operation x2 -> x0, loops' own time: 94.2 us -> none  [apply_tasks(): lax.scan(one_task, start, (left_env, right_env, in_sector, out_sector))]
    pallas_call x0 -> x1, Pallas kernels: none -> 76 us  [per_device(): pl.pallas_call(functools.partial(kernel, S, T), out_shape=(jax.ShapeDtype...]
    dot_general x48 -> x0, matrix products: 66.1 us -> none  [the longest x24 33.9 us: one_task(): jnp.dot(left, block, precision=lax.Precision.HIGHEST, preferred_element_t...]
    unnamed x8 -> x0, waiting for transfers between devices: 56.8 us -> none
    all_gather x2 -> x0, waiting for transfers between devices: 55 us -> none  [the longest x1 31.1 us: per_device(): full = lax.all_gather(wavefunction, 'sector', axis=0, tiled=True)]
    dynamic_slice x72 -> x0, local copies, waits for them, and re-layouts: 44.6 us -> none  [the longest x48 44 us: apply_tasks(): lax.scan(one_task, start, (left_env, right_env, in_sector, out_sector))]
    psum x2 -> x0, blocking collectives: 20.9 us -> none  [per_device(): res_total, upd_total = lax.psum((res_sq, upd_sq), 'sector')]
  transfers between devices with their start and end apart: 6 -> 0, of which waited for: 6 -> 0; matrix products, arithmetic and copies ran while one was open for 0% -> 0% of each run, Pallas kernels for 0% -> 0%
where the time goes in v1:
time: 79.8 us; the launch traced here: 79.4 us
  Pallas kernels  76 us (95%)
  local copies, waits for them, and re-layouts  2.8 us (4%)
    pallas_call x1, Pallas kernels, per_device(): pl.pallas_call(functools.partial(kernel, S, T), out_shape=(jax.ShapeDtype...  76 us
    unnamed x2, local copies, waits for them, and re-layouts  2.8 us

profile of v1, /device:TPU:0, one launch (start us, length us, event | category | flops | bytes accessed | tf_op | source)
XLA Modules:
  0.0 79.4 jit_solution(8060120084813088880)
XLA Ops:
  0.6 76.0 %shard_map.86 = (f32[1,256,256]{2,1,0:T(8,128)}, f32[2]{0:T(128)}) custom-call(s32[12]{0:T(128)} %in_s.1, s32[12]{0:T(128)} %out_s.1, f32[2]{0:T(128)} %shifts.1, f32[1,256,256]{2,1,0:T(8,128)} %wf.1, f32[1,256,256]{2,1,0:T(8,128)} %pre.1, f32[12,256,256]{2,1,0:T(8,128)} %left.1, f32[12,256,256]{2,1,0:T(8,128)} %right.1), custom_call_target="tpu_custom_call" | custom-call | tf_op jit(solution)/shard_map/pallas_call | solution.py:373
  76.6 1.7 %copy.11 = f32[1,256,256]{2,1,0:T(8,128)} copy(f32[1,256,256]{2,1,0:T(8,128)} %get-tuple-element.4) | data formatting | bytes 524288
  78.3 1.1 %copy.12 = f32[2]{0:T(128)} copy(f32[2]{0:T(128)} %get-tuple-element.5) | data formatting | bytes 16

commit v2 on v1

--- a/solution.py
+++ b/solution.py
@@ -16,29 +16,33 @@
     return hi, (x - hi.astype(F32)).astype(BF16)
 
 
-def rcopy(src, dst, sems, at, dev):
+def rcopy(src, dst, sems, out_at, in_at, dev):
     return pltpu.make_async_remote_copy(
         src_ref=src,
         dst_ref=dst,
-        send_sem=sems[0].at[at],
-        recv_sem=sems[1].at[at],
+        send_sem=sems[0].at[out_at],
+        recv_sem=sems[1].at[in_at],
         device_id=dev,
         device_id_type=pl.DeviceIdType.MESH,
     )
 
 
 def each(start, stop, body):
-    lax.fori_loop(start, stop, lambda i, _: (body(i), 0)[1], 0)
+    if stop - start <= 4:
+        for i in range(start, stop):
+            body(i)
+    else:
+        lax.fori_loop(start, stop, lambda i, _: (body(i), 0)[1], 0)
 
 
 def kernel(
     S, T,
     in_s, out_s, shifts, wf, pre, left, right,
     out, norms,
-    stage, env, full, fin, psi, mid, res, part, p1r, p2r, zsum, p3r, stat, zsr, xsr, csr,
+    stage, env, full, fin, psi, mid, res, part, p1r, p2r, zsum, p3r, stat, zsr, xsr,
     esem, *sems,
 ):
-    g0, f0, p1, p2, p3, zg, xg, cg, zst, xst, cst = [
+    g0, f0, p1, p2, p3, zg, xg, cg, zst, xst = [
         (sems[2 * i], sems[2 * i + 1]) for i in range(len(sems) // 2)
     ]
     n_task, B = left.shape[0], wf.shape[-1]
@@ -67,6 +71,9 @@
     def z_dev(k):
         return (ms, z_to(k) * 2 + mc)
 
+    def term_dev(k):
+        return (ms, lax.rem(mt + k, T))
+
     core_dev = (ms, mz * 2 + 1 - mc)
 
     def half(c):
@@ -91,24 +98,24 @@
         pl.semaphore_signal(barrier, inc=1, device_id=dev, device_id_type=pl.DeviceIdType.MESH)
 
     each(1, S, lambda k: greet(xy_dev(k)))
-    each(1, Z, lambda k: greet(z_dev(k)))
-    greet(core_dev)
-    pl.semaphore_wait(barrier, S + Z - 1)
+    for k in range(1, T):
+        greet(term_dev(k))
+    pl.semaphore_wait(barrier, S + T - 2)
 
     def g0_copy(k):
-        return rcopy(wf.at[0, half(mc)], full.at[0, ms, half(mc)], g0, k, xy_dev(k))
+        return rcopy(wf.at[0, half(mc)], full.at[0, ms, half(mc)], g0, 0, k, xy_dev(k))
 
     def g0_in(k):
         here = full.at[0, sec_from(k), half(mc)]
-        return rcopy(here, here, g0, k, xy_dev(k))
+        return rcopy(here, here, g0, 0, k, xy_dev(k))
 
     def f0_copy(k):
         here = full.at[0, sec_from(k), half(mc)]
-        return rcopy(here, here, f0, k, core_dev)
+        return rcopy(here, here, f0, 0, k, core_dev)
 
     def f0_in(k):
         here = full.at[0, sec_from(k), half(1 - mc)]
-        return rcopy(here, here, f0, k, core_dev)
+        return rcopy(here, here, f0, 0, k, core_dev)
 
     each(1, S, lambda k: g0_copy(k).start())
 
@@ -145,7 +152,7 @@
 
     each(1, S, arrive0)
 
-    scale = None
+    tile = jnp.zeros((8, 128), F32)
     for it in range(iters):
         last = it == iters - 1
 
@@ -169,8 +176,10 @@
                 preferred_element_type=F32,
             )
 
-        each(0, n_task, first)
-        each(0, n_task, second)
+        for t in range(n_task):
+            first(t)
+        for t in range(n_task):
+            second(t)
 
         def sums(s, c, dst, extra):
             coef = [jnp.where(out_s[t] == s, 1.0, 0.0).astype(F32) for t in range(n_task)]
@@ -188,7 +197,7 @@
             each(0, H // CH, rows)
 
         def p1_copy(s):
-            return rcopy(part.at[1, s], p1r.at[it, s], p1, (it, s), core_dev)
+            return rcopy(part.at[1, s], p1r.at[it, s], p1, it, (it, s), core_dev)
 
         def to_partner(k):
             s = sec_to(k)
@@ -199,7 +208,7 @@
 
         def p2_copy(j, k):
             return rcopy(
-                part.at[0, sec_to(j), zrows(z_to(k))], p2r.at[it, j, k], p2, (it, j, k), xy_dev(j)
+                part.at[0, sec_to(j), zrows(z_to(k))], p2r.at[it, k, j], p2, it, (it, k), xy_dev(j)
             )
 
         def to_owner(j):
@@ -214,13 +223,14 @@
 
         def piece_sum(k):
             total = part[0, ms, zrows(z_to(k)), :]
+            here = p2r.at[it, k, pl.ds(1, S - 1)]
+            rcopy(here, here, p2, it, (it, k), xy_dev(1)).wait_recv()
             for j in range(1, S):
-                p2_copy(j, k).wait_recv()
-                total = total + p2r[it, j, k]
+                total = total + p2r[it, k, j]
             return total
 
         def p3_copy(k):
-            return rcopy(zsum.at[k], p3r.at[it, k], p3, (it, k), z_dev(k))
+            return rcopy(zsum.at[k], p3r.at[it, k], p3, it, (it, k), z_dev(k))
 
         def to_z(k):
             zsum[k] = piece_sum(k)
@@ -240,7 +250,7 @@
         res_sq = jnp.sum(residual * residual, axis=(0, 1), keepdims=True)
         upd_sq = jnp.sum(updated * updated, axis=(0, 1), keepdims=True)
         row = lax.broadcasted_iota(jnp.int32, (8, 128), 0)
-        tile = jnp.where(row < 4, res_sq, upd_sq)
+        tile = tile + jnp.where(row == 2 * it, res_sq, 0.0) + jnp.where(row == 2 * it + 1, upd_sq, 0.0)
 
         def spot(s, at):
             return fin.at[at] if last else full.at[it + 1, s, at]
@@ -249,64 +259,60 @@
             fin[mine, :] = updated
         else:
             full[it + 1, ms, mine, :] = updated
-        stat[it, 0] = tile
+        if last:
+            stat[0] = tile
 
         def zst_copy(k):
-            return rcopy(stat.at[it, 0], zsr.at[it, k], zst, (it, k), z_dev(k))
+            return rcopy(stat.at[0], zsr.at[k], zst, 0, k, term_dev(k))
 
         def xst_copy(j):
-            return rcopy(stat.at[it, 1], xsr.at[it, j], xst, (it, j), xy_dev(j))
-
-        cst_copy = rcopy(stat.at[it, 2], csr.at[it], cst, it, core_dev)
+            return rcopy(stat.at[1], xsr.at[j], xst, 0, j, xy_dev(j))
 
         def zg_copy(k):
-            return rcopy(spot(ms, mine), spot(ms, mine), zg, (it, k), z_dev(k))
+            return rcopy(spot(ms, mine), spot(ms, mine), zg, it, (it, k), z_dev(k))
 
         def zg_in(k):
             here = spot(ms, piece(mc, z_from(k)))
-            return rcopy(here, here, zg, (it, k), z_dev(k))
+            return rcopy(here, here, zg, it, (it, k), z_dev(k))
 
         def xg_copy(j, k):
             here = spot(ms, piece(mc, z_from(k)))
-            return rcopy(here, here, xg, (it, j, k), xy_dev(j))
+            return rcopy(here, here, xg, it, (it, j, k), xy_dev(j))
 
         def xg_in(j, k):
             here = spot(sec_from(j), piece(mc, z_from(k)))
-            return rcopy(here, here, xg, (it, j, k), xy_dev(j))
+            return rcopy(here, here, xg, it, (it, j, k), xy_dev(j))
 
         def cg_copy(j, k):
             here = spot(sec_from(j), piece(mc, z_from(k)))
-            return rcopy(here, here, cg, (it, j, k), core_dev)
-
-        def cg_in(j, k):
-            here = spot(sec_from(j), piece(1 - mc, z_from(k)))
-            return rcopy(here, here, cg, (it, j, k), core_dev)
+            return rcopy(here, here, cg, it, (it, j), core_dev)
+
+        def cg_in(j):
+            here = spot(sec_from(j), half(1 - mc))
+            return rcopy(here, here, cg, it, (it, j), core_dev)
 
         def spread(k):
             if not last:
                 each(1, S, lambda j: xg_copy(j, k).start())
             cg_copy(0, k).start()
 
-        each(1, Z, lambda k: zst_copy(k).start())
+        if last:
+            for k in range(1, T):
+                zst_copy(k).start()
         each(1, Z, lambda k: zg_copy(k).start())
         spread(0)
-        for k in range(1, Z):
-            zst_copy(k).wait_recv()
-            tile = tile + zsr[it, k]
-        stat[it, 1] = tile
-        each(1, S, lambda j: xst_copy(j).start())
+        if last:
+            for k in range(1, T):
+                zst_copy(k).wait_recv()
+                tile = tile + zsr[k]
+            stat[1] = tile
+            each(1, S, lambda j: xst_copy(j).start())
 
         def relay_z(k):
             zg_in(k).wait_recv()
             spread(k)
 
         each(1, Z, relay_z)
-
-        for j in range(1, S):
-            xst_copy(j).wait_recv()
-            tile = tile + xsr[it, j]
-        stat[it, 2] = tile
-        cst_copy.start()
 
         if not last:
             def relay_xy(k):
@@ -318,43 +324,45 @@
 
             each(0, Z, relay_xy)
 
-        cst_copy.wait_recv()
-        tile = tile + csr[it]
-        res_all, upd_all = tile[0:1, 0:1], tile[4:5, 0:1]
-        norm = jnp.sqrt(res_all)
-        mean = upd_all / count
-        if scale is None:
-            scale = 1.0 / jnp.sqrt(mean + 1e-06)
-        else:
-            norm = norm * scale
-            scale = scale / jnp.sqrt(scale * scale * mean + 1e-06)
-        norms[it] = norm[0, 0]
-
-        if last:
-            each(0, Z, lambda k: cg_in(0, k).wait_recv())
+        if last:
+            for j in range(1, S):
+                xst_copy(j).wait_recv()
+                tile = tile + xsr[j]
+            scale = jnp.ones((1, 1), F32)
+            for n in range(iters):
+                norms[n] = (scale * jnp.sqrt(tile[2 * n : 2 * n + 1, 0:1]))[0, 0]
+                mean = tile[2 * n + 1 : 2 * n + 2, 0:1] / count
+                scale = scale / jnp.sqrt(scale * scale * mean + 1e-06)
+            cg_in(0).wait_recv()
             out[0] = fin[...] * scale
         else:
             def arrive(j):
-                each(0, Z, lambda k: cg_in(j, k).wait_recv())
+                cg_in(j).wait_recv()
                 s = sec_from(j)
                 split_rows(lambda at: full[it + 1, s, at, :], psi, s)
 
             each(0, S, arrive)
 
+        def sent(size, kind, at):
+            rcopy(size, size, kind, at, kind_at[len(kind[1].shape)], core_dev).wait_send()
+
+        kind_at = {1: 0, 2: (0, 0), 3: (0, 0, 0)}
+        others = part.at[0, pl.ds(0, S - 1)]
+        rows_out = zsum.at[pl.ds(0, Z - 1)]
         if it == 0:
-            each(1, S, lambda k: g0_copy(k).wait_send())
-            each(1, S, lambda k: f0_copy(k).wait_send())
-        each(0, S, lambda s: p1_copy(s).wait_send())
-        each(1, S, lambda j: each(0, Z, lambda k: p2_copy(j, k).wait_send()))
-        each(1, Z, lambda k: p3_copy(k).wait_send())
-        each(1, Z, lambda k: zst_copy(k).wait_send())
-        each(1, S, lambda j: xst_copy(j).wait_send())
-        cst_copy.wait_send()
-        each(1, Z, lambda k: zg_copy(k).wait_send())
-        each(0, Z, lambda k: cg_copy(0, k).wait_send())
-        if not last:
-            each(1, S, lambda j: each(0, Z, lambda k: xg_copy(j, k).wait_send()))
-            each(1, S, lambda j: each(0, Z, lambda k: cg_copy(j, k).wait_send()))
+            sent(others, g0, 0)
+            sent(others, f0, 0)
+        sent(part.at[1], p1, it)
+        sent(others, p2, it)
+        sent(rows_out, p3, it)
+        sent(rows_out, zg, it)
+        if last:
+            sent(part.at[0, 0], cg, it)
+            sent(zsr.at[pl.ds(0, T - 1)], zst, 0)
+            sent(xsr.at[pl.ds(0, S - 1)], xst, 0)
+        else:
+            sent(others, xg, it)
+            sent(part.at[0], cg, it)
 
 
 def per_device(S, T, wavefunction, left_env, right_env, in_sector, out_sector, precond, shifts):
@@ -367,8 +375,8 @@
     smem = pl.BlockSpec(memory_space=pltpu.SMEM)
     hbm = pl.BlockSpec(memory_space=pl.ANY)
     sem_shapes = [
-        (S,), (S,), (iters, S), (iters, S, Z), (iters, Z), (iters, Z),
-        (iters, S, Z), (iters, S, Z), (iters, Z), (iters, S), (iters,),
+        (1,), (S,), (1,), (S,), (iters,), (iters, S), (iters,), (iters, Z), (iters,), (iters, Z),
+        (iters,), (iters, Z), (iters,), (iters, S, Z), (iters,), (iters, S), (1,), (T,), (1,), (S,),
     ]
     return pl.pallas_call(
         functools.partial(kernel, S, T),
@@ -388,16 +396,15 @@
             pltpu.VMEM((n_task, B, B), F32),
             pltpu.VMEM((2, S, H, B), F32),
             pltpu.VMEM((iters, S, H, B), F32),
-            pltpu.VMEM((iters, S, Z, R, B), F32),
+            pltpu.VMEM((iters, Z, S, R, B), F32),
             pltpu.VMEM((Z, R, B), F32),
             pltpu.VMEM((iters, Z, R, B), F32),
-            pltpu.VMEM((iters, 3, 8, 128), F32),
-            pltpu.VMEM((iters, Z, 8, 128), F32),
-            pltpu.VMEM((iters, S, 8, 128), F32),
-            pltpu.VMEM((iters, 8, 128), F32),
+            pltpu.VMEM((2, 8, 128), F32),
+            pltpu.VMEM((T, 8, 128), F32),
+            pltpu.VMEM((S, 8, 128), F32),
             dma((2, n_task)),
         ]
-        + [dma(shape) for shape in sem_shapes for _ in range(2)],
+        + [dma(shape) for shape in sem_shapes],
         compiler_params=pltpu.CompilerParams(
             collective_id=0, has_side_effects=True, vmem_limit_bytes=62 * 1024 * 1024
         ),

time: 79.8 us -> 69.3 us (0.87)
  Pallas kernels: 76 us -> 65.7 us
    pallas_call x1, Pallas kernels: 76 us -> 65.7 us  [per_device(): pl.pallas_call(functools.partial(kernel, S, T), out_shape=(jax.ShapeDtype...]
where the time goes in v2:
time: 69.3 us; the launch traced here: 69.2 us
  Pallas kernels  65.7 us (95%)
  local copies, waits for them, and re-layouts  2.8 us (4%)
    pallas_call x1, Pallas kernels, per_device(): pl.pallas_call(functools.partial(kernel, S, T), out_shape=(jax.ShapeDtype...  65.7 us
    unnamed x2, local copies, waits for them, and re-layouts  2.8 us

profile of v2, /device:TPU:0, one launch (start us, length us, event | category | flops | bytes accessed | tf_op | source)
XLA Modules:
  0.0 69.2 jit_solution(2170979706980348511)
XLA Ops:
  0.6 65.7 %shard_map.86 = (f32[1,256,256]{2,1,0:T(8,128)}, f32[2]{0:T(128)}) custom-call(s32[12]{0:T(128)} %in_s.1, s32[12]{0:T(128)} %out_s.1, f32[2]{0:T(128)} %shifts.1, f32[1,256,256]{2,1,0:T(8,128)} %wf.1, f32[1,256,256]{2,1,0:T(8,128)} %pre.1, f32[12,256,256]{2,1,0:T(8,128)} %left.1, f32[12,256,256]{2,1,0:T(8,128)} %right.1), custom_call_target="tpu_custom_call" | custom-call | tf_op jit(solution)/shard_map/pallas_call | solution.py:381
  66.4 1.7 %copy.11 = f32[1,256,256]{2,1,0:T(8,128)} copy(f32[1,256,256]{2,1,0:T(8,128)} %get-tuple-element.4) | data formatting | bytes 524288
  68.0 1.1 %copy.12 = f32[2]{0:T(128)} copy(f32[2]{0:T(128)} %get-tuple-element.5) | data formatting | bytes 16

commit v3 on v2

--- a/solution.py
+++ b/solution.py
@@ -68,6 +68,9 @@
     def xy_dev(k):
         return (sec_to(k), mt)
 
+    def far(k):
+        return lax.rem(jnp.where(mz < Z // 2, Z - k, k), Z)
+
     def z_dev(k):
         return (ms, z_to(k) * 2 + mc)
 
@@ -89,9 +92,6 @@
         src = left if which == 0 else right
         return pltpu.make_async_copy(src.at[t], stage.at[which, t], esem.at[which, t])
 
-    for which in range(2):
-        each(0, n_task, lambda t: env_copy(which, t).start())
-
     barrier = pltpu.get_barrier_semaphore()
 
     def greet(dev):
@@ -100,24 +100,9 @@
     each(1, S, lambda k: greet(xy_dev(k)))
     for k in range(1, T):
         greet(term_dev(k))
-    pl.semaphore_wait(barrier, S + T - 2)
-
-    def g0_copy(k):
-        return rcopy(wf.at[0, half(mc)], full.at[0, ms, half(mc)], g0, 0, k, xy_dev(k))
-
-    def g0_in(k):
-        here = full.at[0, sec_from(k), half(mc)]
-        return rcopy(here, here, g0, 0, k, xy_dev(k))
-
-    def f0_copy(k):
-        here = full.at[0, sec_from(k), half(mc)]
-        return rcopy(here, here, f0, 0, k, core_dev)
-
-    def f0_in(k):
-        here = full.at[0, sec_from(k), half(1 - mc)]
-        return rcopy(here, here, f0, 0, k, core_dev)
-
-    each(1, S, lambda k: g0_copy(k).start())
+
+    for which in range(2):
+        each(0, n_task, lambda t: env_copy(which, t).start())
 
     CH = 32
 
@@ -131,6 +116,25 @@
         each(0, B // CH, rows)
 
     split_rows(lambda at: wf[0, at, :], psi, ms)
+
+    pl.semaphore_wait(barrier, S + T - 2)
+
+    def g0_copy(k):
+        return rcopy(wf.at[0, half(mc)], full.at[0, ms, half(mc)], g0, 0, k, xy_dev(k))
+
+    def g0_in(k):
+        here = full.at[0, sec_from(k), half(mc)]
+        return rcopy(here, here, g0, 0, k, xy_dev(k))
+
+    def f0_copy(k):
+        here = full.at[0, sec_from(k), half(mc)]
+        return rcopy(here, here, f0, 0, k, core_dev)
+
+    def f0_in(k):
+        here = full.at[0, sec_from(k), half(1 - mc)]
+        return rcopy(here, here, f0, 0, k, core_dev)
+
+    each(1, S, lambda k: g0_copy(k).start())
 
     for which in range(2):
         def convert(t):
@@ -215,9 +219,10 @@
             s = sec_to(j)
             p1_copy(s).wait_recv()
             sums(s, mc, 0, True)
-            each(1, Z + 1, lambda k: p2_copy(j, lax.rem(k, Z)).start())
 
         each(1, S, to_owner)
+        for k in range(1, Z + 1):
+            each(1, S, lambda j: p2_copy(j, far(k)).start())
         p1_copy(ms).wait_recv()
         sums(ms, mc, 0, True)
 
@@ -236,7 +241,7 @@
             zsum[k] = piece_sum(k)
             p3_copy(k).start()
 
-        each(1, Z, to_z)
+        each(1, Z, lambda k: to_z(far(k)))
         sigma = piece_sum(0)
         for k in range(1, Z):
             p3_copy(k).wait_recv()
@@ -299,7 +304,7 @@
         if last:
             for k in range(1, T):
                 zst_copy(k).start()
-        each(1, Z, lambda k: zg_copy(k).start())
+        each(1, Z, lambda k: zg_copy(far(k)).start())
         spread(0)
         if last:
             for k in range(1, T):
@@ -312,7 +317,7 @@
             zg_in(k).wait_recv()
             spread(k)
 
-        each(1, Z, relay_z)
+        each(1, Z, lambda k: relay_z(far(k)))
 
         if not last:
             def relay_xy(k):
@@ -322,7 +327,8 @@
 
                 each(1, S, one)
 
-            each(0, Z, relay_xy)
+            relay_xy(0)
+            each(1, Z, lambda k: relay_xy(far(k)))
 
         if last:
             for j in range(1, S):

time: 69.3 us -> 66.7 us (0.962)
  Pallas kernels: 65.7 us -> 63 us
    pallas_call x1, Pallas kernels: 65.7 us -> 63 us  [per_device(): pl.pallas_call(functools.partial(kernel, S, T), out_shape=(jax.ShapeDtype...]
where the time goes in v3:
time: 66.7 us; the launch traced here: 66.5 us
  Pallas kernels  63 us (94%)
  local copies, waits for them, and re-layouts  2.8 us (4%)
    pallas_call x1, Pallas kernels, per_device(): pl.pallas_call(functools.partial(kernel, S, T), out_shape=(jax.ShapeDtype...  63 us
    unnamed x2, local copies, waits for them, and re-layouts  2.8 us

profile of v3, /device:TPU:0, one launch (start us, length us, event | category | flops | bytes accessed | tf_op | source)
XLA Modules:
  0.0 66.5 jit_solution(2499251979190776263)
XLA Ops:
  0.6 63.0 %shard_map.86 = (f32[1,256,256]{2,1,0:T(8,128)}, f32[2]{0:T(128)}) custom-call(s32[12]{0:T(128)} %in_s.1, s32[12]{0:T(128)} %out_s.1, f32[2]{0:T(128)} %shifts.1, f32[1,256,256]{2,1,0:T(8,128)} %wf.1, f32[1,256,256]{2,1,0:T(8,128)} %pre.1, f32[12,256,256]{2,1,0:T(8,128)} %left.1, f32[12,256,256]{2,1,0:T(8,128)} %right.1), custom_call_target="tpu_custom_call" | custom-call | tf_op jit(solution)/shard_map/pallas_call | solution.py:387
  63.7 1.7 %copy.11 = f32[1,256,256]{2,1,0:T(8,128)} copy(f32[1,256,256]{2,1,0:T(8,128)} %get-tuple-element.4) | data formatting | bytes 524288
  65.4 1.1 %copy.12 = f32[2]{0:T(128)} copy(f32[2]{0:T(128)} %get-tuple-element.5) | data formatting | bytes 16
